TPU v7x, 32 devices: a whole 2x2x4 slice. The times are simulated.
32 devices in a mesh: sub: 8 (over y, x, core), front: 4 (over z).
Axes of the slice: x: 2, y: 2, z: 4, core: 2. Of those that a mesh axis runs over, the one named last changes fastest.
Arguments:
- front_inverse: bfloat16 [8, 8192, 2048], P('sub', 'front'), may hold values from -0.75 to 0.75
- coupling: bfloat16 [8, 8192, 2048], P('sub', 'front'), may hold values from -0.0234375 to 0.0234375
- free_modes: bfloat16 [8, 300, 8192], P('sub', None, 'front'), may hold values from -0.125 to 0.125
- dof_offset: int32 [8, 256], P('sub', 'front'), may hold values from 0 to 2047, as said below
- interface_id: int32 [8, 256], replicated, may hold values from 0 to 1023, as said below
Outputs:
- attachment: bfloat16 [8, 256, 8192], P('sub', None, 'front')
- flexibility: float32 [1024, 1024], P(('sub', 'front'))
Inputs may be any that keep to these rules, and one draw needn't show every extreme that they name: `dof_offset`: within one substructure and one front the 64 offsets are distinct, and 0 and 2047 occur among them. `interface_id`: every value occurs exactly twice in the whole array.
All inputs are finite; a program needn't handle non-finite values.
Results may differ from a plain program's by a relative error of at most 0.02.
Values may be sent and summed in bfloat16 or wider, within the bound.
No kernel may reach another device: no remote copies, remote signals or barrier semaphores. Data moves between devices by JAX's collectives and lax.ppermute only.
A program may use at most 128 MiB of HBM per device.

v0:
```python
import jax
import jax.numpy as jnp
from jax import lax
from jax.sharding import PartitionSpec as P


def shifted(value, axis, steps):
    count = lax.axis_size(axis)
    leading, last = (max(0, -steps), min(count, count - steps))
    return lax.ppermute(value, axis, [(source, source + steps) for source in range(leading, last)])


def contract_last(left, right):
    return lax.dot_general(
        left, right, (((1,), (1,)), ((), ())), preferred_element_type=jnp.float32
    )


def on_device(front_inverse, coupling, free_modes, dof_offset, interface_id):
    inverse_block = front_inverse[0]
    coupling_block = coupling[0]
    mode_block = free_modes[0]
    offsets = dof_offset[0]
    order = inverse_block.shape[0]
    columns_all = interface_id.shape[1]
    per_front = offsets.shape[0]
    fronts = lax.axis_size("front")
    front_pos = lax.axis_index("front")
    sub_pos = lax.axis_index("sub")
    column_ids = jnp.arange(columns_all, dtype=jnp.int32)
    local_ids = jnp.arange(per_front, dtype=jnp.int32)
    row_ids = jnp.arange(order, dtype=jnp.int32)
    column_pick = (column_ids[:, None] == front_pos * per_front + local_ids[None, :]).astype(
        jnp.float32
    )
    row_pick = (offsets[:, None] == row_ids[None, :]).astype(jnp.float32)
    forces = jnp.dot(column_pick, row_pick, precision=lax.Precision.HIGHEST)
    groups = 1
    width = columns_all // groups
    force_groups = forces.reshape(groups, width, order)
    moments = groups + fronts - 1

    def forward(moment, carry):
        solved, outgoing = carry
        incoming = shifted(outgoing, "front", 1)
        panel = moment - front_pos
        valid = (panel >= 0) & (panel < groups)
        clipped = jnp.clip(panel, 0, groups - 1)

        def forward_active(unused):
            load = lax.dynamic_index_in_dim(force_groups, clipped, 0, keepdims=False)
            reduced = (load - contract_last(incoming, coupling_block)).astype(jnp.bfloat16)
            return contract_last(reduced, inverse_block).astype(jnp.bfloat16)

        def forward_waiting(unused):
            return outgoing

        result = lax.cond(valid, forward_active, forward_waiting, 0)
        solved = lax.dynamic_update_index_in_dim(solved, result, clipped, 0)
        return (solved, result)

    forward_start = (
        jnp.zeros((groups, width, order), jnp.bfloat16),
        jnp.zeros((width, order), jnp.bfloat16),
    )
    solved, forward_last = lax.fori_loop(0, moments, forward, forward_start)

    def backward(moment, carry):
        moved, outgoing = carry
        incoming = shifted(outgoing, "front", -1)
        panel = moment - (fronts - 1 - front_pos)
        valid = (panel >= 0) & (panel < groups)
        clipped = jnp.clip(panel, 0, groups - 1)

        def backward_active(unused):
            upper = lax.dynamic_index_in_dim(solved, clipped, 0, keepdims=False).astype(jnp.float32)
            reduced = (upper - incoming.astype(jnp.float32)).astype(jnp.bfloat16)
            displaced = jnp.dot(reduced, inverse_block, preferred_element_type=jnp.float32)
            handed = jnp.dot(
                displaced.astype(jnp.bfloat16), coupling_block, preferred_element_type=jnp.float32
            )
            return (displaced, handed.astype(jnp.bfloat16))

        def backward_waiting(unused):
            return (lax.dynamic_index_in_dim(moved, clipped, 0, keepdims=False), outgoing)

        displaced, handed = lax.cond(valid, backward_active, backward_waiting, 0)
        moved = lax.dynamic_update_index_in_dim(moved, displaced, clipped, 0)
        return (moved, handed)

    backward_start = (
        jnp.zeros((groups, width, order), jnp.float32),
        jnp.zeros((width, order), jnp.bfloat16),
    )
    moved, backward_last = lax.fori_loop(0, moments, backward, backward_start)
    displacement = moved.reshape(columns_all, order)
    modal = lax.psum(
        contract_last(displacement.astype(jnp.bfloat16), mode_block).astype(jnp.bfloat16), "front"
    )
    deflated = displacement - jnp.dot(modal, mode_block, preferred_element_type=jnp.float32)
    own_rows = jnp.take(deflated, offsets, axis=1).T
    total_ids = interface_id.shape[0] * columns_all // 2
    dual_ids = jnp.arange(total_ids, dtype=jnp.int32)
    owners = lax.axis_size("sub") * fronts
    share = total_ids // owners
    gathered = lax.all_gather(
        own_rows.astype(jnp.bfloat16), ("sub", "front"), axis=0, tiled=True
    ).astype(own_rows.dtype)
    subs_all = interface_id.shape[0]
    flat_labels = interface_id.reshape(-1)
    owner_pos = sub_pos * fronts + front_pos
    targets = owner_pos * share + jnp.arange(share, dtype=jnp.int32)
    row_select = (targets[:, None] == flat_labels[None, :]).astype(jnp.float32)
    reduced = jnp.einsum(
        "asc,scd->asd",
        row_select.reshape(share, subs_all, columns_all),
        gathered.reshape(subs_all, columns_all, columns_all),
        precision=lax.Precision.HIGHEST,
    )
    column_place = (flat_labels[:, None] == dual_ids[None, :]).astype(jnp.float32)
    flexibility = jnp.dot(
        reduced.reshape(share, subs_all * columns_all),
        column_place,
        precision=lax.Precision.HIGHEST,
    )
    return (deflated.astype(jnp.bfloat16)[None], flexibility)


def solution(mesh):
    return jax.shard_map(
        on_device,
        mesh=mesh,
        in_specs=(
            P("sub", "front", None),
            P("sub", "front", None),
            P("sub", None, "front"),
            P("sub", "front"),
            P(),
        ),
        out_specs=(P("sub", None, "front"), P(("sub", "front"), None)),
        check_vma=False,
    )
```

profile of v0, /device:TPU:0, one launch (start us, length us, event | category | flops | bytes accessed | tf_op | source)
XLA Modules:
  0.0 390.6 jit_solution(3004368580467127556)
XLA Ops:
  7.3 2.6 convolution_bitcast_fusion
  9.9 126.6 %while.35 = (s32[]{:T(128)}, bf16[1,256,2048]{2,1,0:T(8,128)(2,1)}, bf16[256,2048]{1,0:T(8,128)(2,1)S(1)}, s32[]{:T(128)}, f32[1,256,2048]{2,1,0:T(8,128)}, /*in...) while((s32[]{:T(128)}, bf16[1,256,2048]{2,1,0:T(8,128)(2,1)}, ...), condition=%wide.region_3.4_spmd, body=%wide.region_0.3_spmd.sunk | while | flops 4296540160 | bytes 33554672 | solution.py:66
  10.1 5.0 %collective-permute-start = (bf16[256,2048]{1,0:T(8,128)(2,1)S(1)}, bf16[256,2048]{1,0:T(8,128)(2,1)S(1)}, u32[]{:S(2)}, u32[]{:S(2)}) collective-permute-start(bf16[256,2048]{1,0:T(8,128)(2,1)S(1)} %copy.23), channel_id=1, source_target_pairs={{0,1},{1,2},{2,3},{4,5},{5,6},{6,7},{8,9},{9,10},{10,11},{12,13},{... | collective-permute-start | bytes 3145736 | tf_op jit(solution)/shard_map/while/body/eval_jaxpr/ppermute | solution.py:10
  15.1 22.3 %collective-permute-done = bf16[256,2048]{1,0:T(8,128)(2,1)S(1)} collective-permute-done((bf16[256,2048]{1,0:T(8,128)(2,1)S(1)}, bf16[256,2048]{1,0:T(8,128)(2,1)S(1)}, u32[]{:S(2)}, u32[]{:S(2)}) %collective-permute-start) | collective-permute-done | bytes 1048608 | tf_op jit(solution)/shard_map/while/body/eval_jaxpr/ppermute | solution.py:10
  37.4 10.9 %conditional.4 = (bf16[256,2048]{1,0:T(8,128)(2,1)S(1)}) conditional(s32[]{:T(128)} %convert_element_type.98, bf16[256,2048]{1,0:T(8,128)(2,1)S(1)} %copy.23, (f32[1,256,2048]{2,1,0:T(8,128)}, bf16[256,2048]{1,0:T(8,128)(2,1)S(1)}, bf16[2048,2048]{1,0:T(8,128)(2,1)}, bf16[2048,2048]{1,0:T(8,128)(2,1)}) %tuple.101), branch_computations={%region_1.1_spmd, %region_2.2_spmd} | conditional | flops 4296540160 | bytes 20971528 | solution.py:58
  37.4 10.9 %convolution_convert_fusion = bf16[256,2048]{1,0:T(8,128)(2,1)S(1)} fusion(bf16[2048,2048]{1,0:T(8,128)(2,1)} %get-tuple-element.340, bf16[256,2048]{1,0:T(8,128)(2,1)S(1)} %get-tuple-element.338, bf16[2048,2048]{1,0:T(8,128)(2,1)} %get-tuple-element.339, f32[1,256,2048]{2,1,0:T(8,128)} %get-tuple-element.337), kind=kOutput, calls=%fused_computation.3 | convolution fusion | flops 4296540160 | bytes 20971520 | tf_op jit(solution)/shard_map/while/body/eval_jaxpr/cond/branch_1_fun/dot_general | solution.py:14
  49.4 1.4 collective-permute-start
  50.8 21.8 %collective-permute-done = bf16[256,2048]{1,0:T(8,128)(2,1)S(1)} collective-permute-done((bf16[256,2048]{1,0:T(8,128)(2,1)S(1)}, bf16[256,2048]{1,0:T(8,128)(2,1)S(1)}, u32[]{:S(2)}, u32[]{:S(2)}) %collective-permute-start) | collective-permute-done | bytes 1048608 | tf_op jit(solution)/shard_map/while/body/eval_jaxpr/ppermute | solution.py:10
  73.6 15.4 %collective-permute-start = (bf16[256,2048]{1,0:T(8,128)(2,1)S(1)}, bf16[256,2048]{1,0:T(8,128)(2,1)S(1)}, u32[]{:S(2)}, u32[]{:S(2)}) collective-permute-start(bf16[256,2048]{1,0:T(8,128)(2,1)S(1)} %copy.23), channel_id=1, source_target_pairs={{0,1},{1,2},{2,3},{4,5},{5,6},{6,7},{8,9},{9,10},{10,11},{12,13},{... | collective-permute-start | bytes 3145736 | tf_op jit(solution)/shard_map/while/body/eval_jaxpr/ppermute | solution.py:10
  89.1 20.9 %collective-permute-done = bf16[256,2048]{1,0:T(8,128)(2,1)S(1)} collective-permute-done((bf16[256,2048]{1,0:T(8,128)(2,1)S(1)}, bf16[256,2048]{1,0:T(8,128)(2,1)S(1)}, u32[]{:S(2)}, u32[]{:S(2)}) %collective-permute-start) | collective-permute-done | bytes 1048608 | tf_op jit(solution)/shard_map/while/body/eval_jaxpr/ppermute | solution.py:10
  111.0 4.5 %collective-permute-start = (bf16[256,2048]{1,0:T(8,128)(2,1)S(1)}, bf16[256,2048]{1,0:T(8,128)(2,1)S(1)}, u32[]{:S(2)}, u32[]{:S(2)}) collective-permute-start(bf16[256,2048]{1,0:T(8,128)(2,1)S(1)} %copy.23), channel_id=1, source_target_pairs={{0,1},{1,2},{2,3},{4,5},{5,6},{6,7},{8,9},{9,10},{10,11},{12,13},{... | collective-permute-start | bytes 3145736 | tf_op jit(solution)/shard_map/while/body/eval_jaxpr/ppermute | solution.py:10
  115.5 20.0 %collective-permute-done = bf16[256,2048]{1,0:T(8,128)(2,1)S(1)} collective-permute-done((bf16[256,2048]{1,0:T(8,128)(2,1)S(1)}, bf16[256,2048]{1,0:T(8,128)(2,1)S(1)}, u32[]{:S(2)}, u32[]{:S(2)}) %collective-permute-start) | collective-permute-done | bytes 1048608 | tf_op jit(solution)/shard_map/while/body/eval_jaxpr/ppermute | solution.py:10
  136.5 1.6 broadcast_in_dim.49
  138.2 144.6 %while.36 = (s32[]{:T(128)}, f32[1,256,2048]{2,1,0:T(8,128)}, bf16[256,2048]{1,0:T(8,128)(2,1)S(1)}, s32[]{:T(128)}, bf16[1,256,2048]{2,1,0:T(8,128)(2,1)S(1)}, ...) while((s32[]{:T(128)}, f32[1,256,2048]{2,1,0:T(8,128)}, ...), condition=%wide.region_7.8_spmd, body=%wide.region_4.7_spmd.sunk | while | flops 4298113024 | bytes 70254888 | solution.py:95
  138.2 1.3 collective-permute-start.1
  139.5 32.5 %collective-permute-done.1 = bf16[256,2048]{1,0:T(8,128)(2,1)} collective-permute-done((bf16[256,2048]{1,0:T(8,128)(2,1)S(1)}, bf16[256,2048]{1,0:T(8,128)(2,1)}, u32[]{:S(2)}, u32[]{:S(2)}) %collective-permute-start.1) | collective-permute-done | bytes 1048608 | tf_op jit(solution)/shard_map/while/body/eval_jaxpr/ppermute | solution.py:10
  172.1 1.3 collective-permute-start.1
  173.4 22.9 %collective-permute-done.1 = bf16[256,2048]{1,0:T(8,128)(2,1)} collective-permute-done((bf16[256,2048]{1,0:T(8,128)(2,1)S(1)}, bf16[256,2048]{1,0:T(8,128)(2,1)}, u32[]{:S(2)}, u32[]{:S(2)}) %collective-permute-start.1) | collective-permute-done | bytes 1048608 | tf_op jit(solution)/shard_map/while/body/eval_jaxpr/ppermute | solution.py:10
  196.3 1.3 collective-permute-start.1
  197.5 31.3 %collective-permute-done.1 = bf16[256,2048]{1,0:T(8,128)(2,1)} collective-permute-done((bf16[256,2048]{1,0:T(8,128)(2,1)S(1)}, bf16[256,2048]{1,0:T(8,128)(2,1)}, u32[]{:S(2)}, u32[]{:S(2)}) %collective-permute-start.1) | collective-permute-done | bytes 1048608 | tf_op jit(solution)/shard_map/while/body/eval_jaxpr/ppermute | solution.py:10
  228.8 1.3 collective-permute-start.1
  230.1 44.1 %collective-permute-done.1 = bf16[256,2048]{1,0:T(8,128)(2,1)} collective-permute-done((bf16[256,2048]{1,0:T(8,128)(2,1)S(1)}, bf16[256,2048]{1,0:T(8,128)(2,1)}, u32[]{:S(2)}, u32[]{:S(2)}) %collective-permute-start.1) | collective-permute-done | bytes 1048608 | tf_op jit(solution)/shard_map/while/body/eval_jaxpr/ppermute | solution.py:10
  274.2 8.5 %conditional.5 = ((bf16[256,2048]{1,0:T(8,128)(2,1)S(1)}, f32[1,256,2048]{2,1,0:T(8,128)})) conditional(s32[]{:T(128)} %convert_element_type.99, (bf16[256,2048]{1,0:T(8,128)(2,1)S(1)}, f32[1,256,2048]{2,1,0:T(8,128)}) %tuple.103, (bf16[1,256,2048]{2,1,0:T(8,128)(2,1)S(1)}, bf16[256,2048]{1,0:T(8,128)(2,1)}, bf16[2048,2048]{1,0:T(8,128)(2,1)}, ...), branch_computations={%region_5.5_spmd, %region_6.6_spmd} | conditional | flops 4298113024 | bytes 66060368 | solution.py:87
  274.2 6.2 %fusion.2 = f32[256,2048]{1,0:T(8,128)S(1)} fusion(bf16[2048,2048]{1,0:T(8,128)(2,1)} %get-tuple-element.350, bf16[256,2048]{1,0:T(8,128)(2,1)} %get-tuple-element.349, bf16[1,256,2048]{2,1,0:T(8,128)(2,1)S(1)} %get-tuple-element.348), kind=kOutput, calls=%fused_computation.7 | convolution fusion | flops 2149580800 | bytes 12582912 | tf_op jit(solution)/shard_map/while/body/eval_jaxpr/cond/branch_1_fun/dot_general | solution.py:78
  280.4 2.3 convolution_convert_fusion.1
  282.8 3.1 fusion.11
  286.3 33.1 %all-reduce.2.cloned.1.call-done = bf16[256,300]{1,0:T(8,128)(2,1)} async-done(((bf16[256,300]{1,0:T(8,128)(2,1)}), bf16[256,300]{1,0:T(8,128)(2,1)}) %all-reduce.2.cloned.1.call-update) | async-done | bytes 153616 | tf_op jit(solution)/shard_map/psum | solution.py:97
  319.4 2.6 convolution_subtract_fusion.1
  322.0 1.5 copy.8
  324.9 53.6 %all-gather.2.cloned.1.call-done = bf16[2048,256]{1,0:T(8,128)(2,1)} async-done(((bf16[64,256]{1,0:T(8,128)(2,1)}), bf16[2048,256]{1,0:T(8,128)(2,1)}) %all-gather.2.cloned.1.call-update) | async-done | bytes 1048592 | tf_op jit(solution)/shard_map/all_gather | solution.py:106
  378.5 1.5 convolution_bitcast_fusion.1
  380.1 3.8 fusion.6
  (52 shorter events, 6.2 us)
Async XLA Ops:
  7.2 275.7 %copy-start = (bf16[1,300,2048]{2,1,0:T(8,128)(2,1)S(1)}, bf16[1,300,2048]{2,1,0:T(8,128)(2,1)}, u32[]{:S(2)}) copy-start(bf16[1,300,2048]{2,1,0:T(8,128)(2,1)} %param.15) | copy-start | bytes 3686404
  7.2 312.2 %all-reduce.2.cloned.1.call-start = ((), (), s32[]{:S(2)}) async-start(), calls=%async_computation | async-start | bytes 393216 | tf_op jit(solution)/shard_map/psum | solution.py:97
  10.1 27.4 %collective-permute-start = (bf16[256,2048]{1,0:T(8,128)(2,1)S(1)}, bf16[256,2048]{1,0:T(8,128)(2,1)S(1)}, u32[]{:S(2)}, u32[]{:S(2)}) collective-permute-start(bf16[256,2048]{1,0:T(8,128)(2,1)S(1)} %copy.23), channel_id=1, source_target_pairs={{0,1},{1,2},{2,3},{4,5},{5,6},{6,7},{8,9},{9,10},{10,11},{12,13},{... | collective-permute-start | bytes 3145736 | tf_op jit(solution)/shard_map/while/body/eval_jaxpr/ppermute | solution.py:10
  48.4 1.0 copy-start.1
  49.4 23.1 %collective-permute-start = (bf16[256,2048]{1,0:T(8,128)(2,1)S(1)}, bf16[256,2048]{1,0:T(8,128)(2,1)S(1)}, u32[]{:S(2)}, u32[]{:S(2)}) collective-permute-start(bf16[256,2048]{1,0:T(8,128)(2,1)S(1)} %copy.23), channel_id=1, source_target_pairs={{0,1},{1,2},{2,3},{4,5},{5,6},{6,7},{8,9},{9,10},{10,11},{12,13},{... | collective-permute-start | bytes 3145736 | tf_op jit(solution)/shard_map/while/body/eval_jaxpr/ppermute | solution.py:10
  72.6 1.0 copy-start.1
  73.6 36.3 %collective-permute-start = (bf16[256,2048]{1,0:T(8,128)(2,1)S(1)}, bf16[256,2048]{1,0:T(8,128)(2,1)S(1)}, u32[]{:S(2)}, u32[]{:S(2)}) collective-permute-start(bf16[256,2048]{1,0:T(8,128)(2,1)S(1)} %copy.23), channel_id=1, source_target_pairs={{0,1},{1,2},{2,3},{4,5},{5,6},{6,7},{8,9},{9,10},{10,11},{12,13},{... | collective-permute-start | bytes 3145736 | tf_op jit(solution)/shard_map/while/body/eval_jaxpr/ppermute | solution.py:10
  110.0 1.0 copy-start.1
  111.0 24.5 %collective-permute-start = (bf16[256,2048]{1,0:T(8,128)(2,1)S(1)}, bf16[256,2048]{1,0:T(8,128)(2,1)S(1)}, u32[]{:S(2)}, u32[]{:S(2)}) collective-permute-start(bf16[256,2048]{1,0:T(8,128)(2,1)S(1)} %copy.23), channel_id=1, source_target_pairs={{0,1},{1,2},{2,3},{4,5},{5,6},{6,7},{8,9},{9,10},{10,11},{12,13},{... | collective-permute-start | bytes 3145736 | tf_op jit(solution)/shard_map/while/body/eval_jaxpr/ppermute | solution.py:10
  135.5 1.0 copy-start.1
  136.5 1.7 copy-start.2
  138.2 33.8 %collective-permute-start.1 = (bf16[256,2048]{1,0:T(8,128)(2,1)S(1)}, bf16[256,2048]{1,0:T(8,128)(2,1)}, u32[]{:S(2)}, u32[]{:S(2)}) collective-permute-start(bf16[256,2048]{1,0:T(8,128)(2,1)S(1)} %get-tuple-element.526), channel_id=1, source_target_pairs={{1,0},{2,1},{3,2},{5,4},{6,5},{7,6},{9,8},{10,9},{11,10},{13,12},{... | collective-permute-start | bytes 3145736 | tf_op jit(solution)/shard_map/while/body/eval_jaxpr/ppermute | solution.py:10
  172.1 24.2 %collective-permute-start.1 = (bf16[256,2048]{1,0:T(8,128)(2,1)S(1)}, bf16[256,2048]{1,0:T(8,128)(2,1)}, u32[]{:S(2)}, u32[]{:S(2)}) collective-permute-start(bf16[256,2048]{1,0:T(8,128)(2,1)S(1)} %get-tuple-element.526), channel_id=1, source_target_pairs={{1,0},{2,1},{3,2},{5,4},{6,5},{7,6},{9,8},{10,9},{11,10},{13,12},{... | collective-permute-start | bytes 3145736 | tf_op jit(solution)/shard_map/while/body/eval_jaxpr/ppermute | solution.py:10
  196.3 32.6 %collective-permute-start.1 = (bf16[256,2048]{1,0:T(8,128)(2,1)S(1)}, bf16[256,2048]{1,0:T(8,128)(2,1)}, u32[]{:S(2)}, u32[]{:S(2)}) collective-permute-start(bf16[256,2048]{1,0:T(8,128)(2,1)S(1)} %get-tuple-element.526), channel_id=1, source_target_pairs={{1,0},{2,1},{3,2},{5,4},{6,5},{7,6},{9,8},{10,9},{11,10},{13,12},{... | collective-permute-start | bytes 3145736 | tf_op jit(solution)/shard_map/while/body/eval_jaxpr/ppermute | solution.py:10
  228.8 45.4 %collective-permute-start.1 = (bf16[256,2048]{1,0:T(8,128)(2,1)S(1)}, bf16[256,2048]{1,0:T(8,128)(2,1)}, u32[]{:S(2)}, u32[]{:S(2)}) collective-permute-start(bf16[256,2048]{1,0:T(8,128)(2,1)S(1)} %get-tuple-element.526), channel_id=1, source_target_pairs={{1,0},{2,1},{3,2},{5,4},{6,5},{7,6},{9,8},{10,9},{11,10},{13,12},{... | collective-permute-start | bytes 3145736 | tf_op jit(solution)/shard_map/while/body/eval_jaxpr/ppermute | solution.py:10
  274.2 6.2 %copy-start.7 = (bf16[2048,2048]{1,0:T(8,128)(2,1)S(1)}, bf16[2048,2048]{1,0:T(8,128)(2,1)}, u32[]{:S(2)}) copy-start(bf16[2048,2048]{1,0:T(8,128)(2,1)} %get-tuple-element.351) | copy-start | bytes 25165828 | tf_op jit(solution)/shard_map/while/body/eval_jaxpr/cond
  280.4 2.4 copy-start.3
  282.8 3.4 copy-start.6
  282.8 36.5 %copy-start.4 = (f32[1,256,2048]{2,1,0:T(8,128)S(1)}, f32[1,256,2048]{2,1,0:T(8,128)}, u32[]{:S(2)}) copy-start(f32[1,256,2048]{2,1,0:T(8,128)} %get-tuple-element.367) | copy-start | bytes 6291460
  286.0 92.5 %all-gather.2.cloned.1.call-start = ((), (), s32[]{:S(2)}) async-start(), calls=%async_computation.1 | async-start | bytes 1081344 | tf_op jit(solution)/shard_map/all_gather | solution.py:106
  322.0 2.9 copy-start.5
Sparse Core Ops, SparseCore 0:
  286.1 33.1 all-reduce.1
  325.0 53.4 all-gather.1
where the time goes:
time: 391 us
  waiting for transfers between devices  302 us (77%)
  matrix products  33 us (8%)
  starting transfers between devices  31.6 us (8%)
  between operations  14.2 us (4%)
  local copies, waits for them, and re-layouts  8.29 us (2%)
    ppermute x8, waiting for transfers between devices, shifted(): lax.ppermute(value, axis, [(source, source + steps) for source in range(l...  216 us
    all_gather x1, waiting for transfers between devices, on_device(): lax.all_gather(own_rows.astype(jnp.bfloat16), ('sub', 'front'), axis=0, t...  53.6 us
    psum x1, waiting for transfers between devices, on_device(): lax.psum(contract_last(displacement.astype(jnp.bfloat16), mode_block).ast...  33.1 us
    ppermute x8, starting transfers between devices, shifted(): lax.ppermute(value, axis, [(source, source + steps) for source in range(l...  31.4 us
    dot_general x2, matrix products, contract_last(): lax.dot_general(left, right, (((1,), (1,)), ((), ())), preferred_element_...  14.1 us
  transfers between devices with their start and end apart: 10, of which 10 were waited for; matrix products, arithmetic and copies ran while one was open for 0% of the time, Pallas kernels for 0%

commit v1 on v0

--- a/solution.py
+++ b/solution.py
@@ -94,9 +94,9 @@
     )
     moved, backward_last = lax.fori_loop(0, moments, backward, backward_start)
     displacement = moved.reshape(columns_all, order)
-    modal = lax.psum(
-        contract_last(displacement.astype(jnp.bfloat16), mode_block).astype(jnp.bfloat16), "front"
-    )
+    block = contract_last(displacement.astype(jnp.bfloat16), mode_block).astype(jnp.bfloat16)
+    terms = lax.all_gather(block, "front", axis=0, tiled=False)
+    modal = terms.sum(axis=0)
     deflated = displacement - jnp.dot(modal, mode_block, preferred_element_type=jnp.float32)
     own_rows = jnp.take(deflated, offsets, axis=1).T
     total_ids = interface_id.shape[0] * columns_all // 2

time: 391 us -> 377 us (0.964)
  waiting for transfers between devices: 302 us -> 268 us
  blocking collectives: 0 us -> 17 us
    psum x1 -> x0, waiting for transfers between devices: 33.1 us -> none  [on_device(): lax.psum(contract_last(displacement.astype(jnp.bfloat16), mode_block).ast...]
    all_gather x0 -> x1, blocking collectives: none -> 17 us  [on_device(): terms = lax.all_gather(block, 'front', axis=0, tiled=False)]
  transfers between devices with their start and end apart: 10 -> 9, of which waited for: 10 -> 9; matrix products, arithmetic and copies ran while one was open for 0% -> 0% of each run, Pallas kernels for 0% -> 0%
where the time goes in v1:
time: 377 us
  waiting for transfers between devices  268 us (71%)
  starting transfers between devices  31.4 us (8%)
  matrix products  31 us (8%)
  blocking collectives  17 us (5%)
  between operations  14.2 us (4%)
  local copies, waits for them, and re-layouts  10.7 us (3%)
  other arithmetic  3.94 us (1%)
    ppermute x8, waiting for transfers between devices, shifted(): lax.ppermute(value, axis, [(source, source + steps) for source in range(l...  216 us
    all_gather x1, waiting for transfers between devices, on_device(): lax.all_gather(own_rows.astype(jnp.bfloat16), ('sub', 'front'), axis=0, t...  52.5 us
    ppermute x8, starting transfers between devices, shifted(): lax.ppermute(value, axis, [(source, source + steps) for source in range(l...  31.4 us
    all_gather x1, blocking collectives, on_device(): terms = lax.all_gather(block, 'front', axis=0, tiled=False)  17 us
    dot_general x2, matrix products, contract_last(): lax.dot_general(left, right, (((1,), (1,)), ((), ())), preferred_element_...  13 us
  transfers between devices with their start and end apart: 9, of which 9 were waited for; matrix products, arithmetic and copies ran while one was open for 0% of the time, Pallas kernels for 0%

profile of v1, /device:TPU:0, one launch (start us, length us, event | category | flops | bytes accessed | tf_op | source)
XLA Modules:
  0.0 376.8 jit_solution(15770255727446597788)
XLA Ops:
  8.7 2.5 convolution_bitcast_fusion
  11.3 126.5 %while.35 = (s32[]{:T(128)}, bf16[1,256,2048]{2,1,0:T(8,128)(2,1)}, bf16[256,2048]{1,0:T(8,128)(2,1)S(1)}, s32[]{:T(128)}, f32[1,256,2048]{2,1,0:T(8,128)}, /*in...) while((s32[]{:T(128)}, bf16[1,256,2048]{2,1,0:T(8,128)(2,1)}, ...), condition=%wide.region_3.4_spmd, body=%wide.region_0.3_spmd.sunk | while | flops 4296540160 | bytes 33554672 | solution.py:66
  11.4 5.0 %collective-permute-start = (bf16[256,2048]{1,0:T(8,128)(2,1)S(1)}, bf16[256,2048]{1,0:T(8,128)(2,1)S(1)}, u32[]{:S(2)}, u32[]{:S(2)}) collective-permute-start(bf16[256,2048]{1,0:T(8,128)(2,1)S(1)} %copy.25), channel_id=1, source_target_pairs={{0,1},{1,2},{2,3},{4,5},{5,6},{6,7},{8,9},{9,10},{10,11},{12,13},{... | collective-permute-start | bytes 3145736 | tf_op jit(solution)/shard_map/while/body/eval_jaxpr/ppermute | solution.py:10
  16.4 22.3 %collective-permute-done = bf16[256,2048]{1,0:T(8,128)(2,1)S(1)} collective-permute-done((bf16[256,2048]{1,0:T(8,128)(2,1)S(1)}, bf16[256,2048]{1,0:T(8,128)(2,1)S(1)}, u32[]{:S(2)}, u32[]{:S(2)}) %collective-permute-start) | collective-permute-done | bytes 1048608 | tf_op jit(solution)/shard_map/while/body/eval_jaxpr/ppermute | solution.py:10
  38.7 10.9 %conditional.4 = (bf16[256,2048]{1,0:T(8,128)(2,1)S(1)}) conditional(s32[]{:T(128)} %convert_element_type.100, bf16[256,2048]{1,0:T(8,128)(2,1)S(1)} %copy.25, (f32[1,256,2048]{2,1,0:T(8,128)}, bf16[256,2048]{1,0:T(8,128)(2,1)S(1)}, bf16[2048,2048]{1,0:T(8,128)(2,1)}, bf16[2048,2048]{1,0:T(8,128)(2,1)}) %tuple.101), branch_computations={%region_1.1_spmd, %region_2.2_spmd} | conditional | flops 4296540160 | bytes 20971528 | solution.py:58
  38.7 10.9 %convolution_convert_fusion = bf16[256,2048]{1,0:T(8,128)(2,1)S(1)} fusion(bf16[2048,2048]{1,0:T(8,128)(2,1)} %get-tuple-element.340, bf16[256,2048]{1,0:T(8,128)(2,1)S(1)} %get-tuple-element.338, bf16[2048,2048]{1,0:T(8,128)(2,1)} %get-tuple-element.339, f32[1,256,2048]{2,1,0:T(8,128)} %get-tuple-element.337), kind=kOutput, calls=%fused_computation.3 | convolution fusion | flops 4296540160 | bytes 20971520 | tf_op jit(solution)/shard_map/while/body/eval_jaxpr/cond/branch_1_fun/dot_general | solution.py:14
  50.8 1.4 collective-permute-start
  52.1 21.7 %collective-permute-done = bf16[256,2048]{1,0:T(8,128)(2,1)S(1)} collective-permute-done((bf16[256,2048]{1,0:T(8,128)(2,1)S(1)}, bf16[256,2048]{1,0:T(8,128)(2,1)S(1)}, u32[]{:S(2)}, u32[]{:S(2)}) %collective-permute-start) | collective-permute-done | bytes 1048608 | tf_op jit(solution)/shard_map/while/body/eval_jaxpr/ppermute | solution.py:10
  74.9 15.4 %collective-permute-start = (bf16[256,2048]{1,0:T(8,128)(2,1)S(1)}, bf16[256,2048]{1,0:T(8,128)(2,1)S(1)}, u32[]{:S(2)}, u32[]{:S(2)}) collective-permute-start(bf16[256,2048]{1,0:T(8,128)(2,1)S(1)} %copy.25), channel_id=1, source_target_pairs={{0,1},{1,2},{2,3},{4,5},{5,6},{6,7},{8,9},{9,10},{10,11},{12,13},{... | collective-permute-start | bytes 3145736 | tf_op jit(solution)/shard_map/while/body/eval_jaxpr/ppermute | solution.py:10
  90.4 20.9 %collective-permute-done = bf16[256,2048]{1,0:T(8,128)(2,1)S(1)} collective-permute-done((bf16[256,2048]{1,0:T(8,128)(2,1)S(1)}, bf16[256,2048]{1,0:T(8,128)(2,1)S(1)}, u32[]{:S(2)}, u32[]{:S(2)}) %collective-permute-start) | collective-permute-done | bytes 1048608 | tf_op jit(solution)/shard_map/while/body/eval_jaxpr/ppermute | solution.py:10
  112.3 4.5 %collective-permute-start = (bf16[256,2048]{1,0:T(8,128)(2,1)S(1)}, bf16[256,2048]{1,0:T(8,128)(2,1)S(1)}, u32[]{:S(2)}, u32[]{:S(2)}) collective-permute-start(bf16[256,2048]{1,0:T(8,128)(2,1)S(1)} %copy.25), channel_id=1, source_target_pairs={{0,1},{1,2},{2,3},{4,5},{5,6},{6,7},{8,9},{9,10},{10,11},{12,13},{... | collective-permute-start | bytes 3145736 | tf_op jit(solution)/shard_map/while/body/eval_jaxpr/ppermute | solution.py:10
  116.8 20.0 %collective-permute-done = bf16[256,2048]{1,0:T(8,128)(2,1)S(1)} collective-permute-done((bf16[256,2048]{1,0:T(8,128)(2,1)S(1)}, bf16[256,2048]{1,0:T(8,128)(2,1)S(1)}, u32[]{:S(2)}, u32[]{:S(2)}) %collective-permute-start) | collective-permute-done | bytes 1048608 | tf_op jit(solution)/shard_map/while/body/eval_jaxpr/ppermute | solution.py:10
  137.8 1.6 broadcast_in_dim.49
  139.5 144.6 %while.36 = (s32[]{:T(128)}, f32[1,256,2048]{2,1,0:T(8,128)}, bf16[256,2048]{1,0:T(8,128)(2,1)S(1)}, s32[]{:T(128)}, bf16[1,256,2048]{2,1,0:T(8,128)(2,1)S(1)}, ...) while((s32[]{:T(128)}, f32[1,256,2048]{2,1,0:T(8,128)}, ...), condition=%wide.region_7.8_spmd, body=%wide.region_4.7_spmd.sunk | while | flops 4298113024 | bytes 70254888 | solution.py:95
  139.5 1.3 collective-permute-start.1
  140.8 32.5 %collective-permute-done.1 = bf16[256,2048]{1,0:T(8,128)(2,1)} collective-permute-done((bf16[256,2048]{1,0:T(8,128)(2,1)S(1)}, bf16[256,2048]{1,0:T(8,128)(2,1)}, u32[]{:S(2)}, u32[]{:S(2)}) %collective-permute-start.1) | collective-permute-done | bytes 1048608 | tf_op jit(solution)/shard_map/while/body/eval_jaxpr/ppermute | solution.py:10
  173.3 1.3 collective-permute-start.1
  174.6 22.9 %collective-permute-done.1 = bf16[256,2048]{1,0:T(8,128)(2,1)} collective-permute-done((bf16[256,2048]{1,0:T(8,128)(2,1)S(1)}, bf16[256,2048]{1,0:T(8,128)(2,1)}, u32[]{:S(2)}, u32[]{:S(2)}) %collective-permute-start.1) | collective-permute-done | bytes 1048608 | tf_op jit(solution)/shard_map/while/body/eval_jaxpr/ppermute | solution.py:10
  198.8 31.3 %collective-permute-done.1 = bf16[256,2048]{1,0:T(8,128)(2,1)} collective-permute-done((bf16[256,2048]{1,0:T(8,128)(2,1)S(1)}, bf16[256,2048]{1,0:T(8,128)(2,1)}, u32[]{:S(2)}, u32[]{:S(2)}) %collective-permute-start.1) | collective-permute-done | bytes 1048608 | tf_op jit(solution)/shard_map/while/body/eval_jaxpr/ppermute | solution.py:10
  231.4 44.1 %collective-permute-done.1 = bf16[256,2048]{1,0:T(8,128)(2,1)} collective-permute-done((bf16[256,2048]{1,0:T(8,128)(2,1)S(1)}, bf16[256,2048]{1,0:T(8,128)(2,1)}, u32[]{:S(2)}, u32[]{:S(2)}) %collective-permute-start.1) | collective-permute-done | bytes 1048608 | tf_op jit(solution)/shard_map/while/body/eval_jaxpr/ppermute | solution.py:10
  275.5 8.6 %conditional.5 = ((bf16[256,2048]{1,0:T(8,128)(2,1)S(1)}, f32[1,256,2048]{2,1,0:T(8,128)})) conditional(s32[]{:T(128)} %convert_element_type.101, (bf16[256,2048]{1,0:T(8,128)(2,1)S(1)}, f32[1,256,2048]{2,1,0:T(8,128)}) %tuple.103, (bf16[1,256,2048]{2,1,0:T(8,128)(2,1)S(1)}, bf16[256,2048]{1,0:T(8,128)(2,1)}, bf16[2048,2048]{1,0:T(8,128)(2,1)}, ...), branch_computations={%region_5.5_spmd, %region_6.6_spmd} | conditional | flops 4298113024 | bytes 66060368 | solution.py:87
  275.5 6.2 %fusion.2 = f32[256,2048]{1,0:T(8,128)S(1)} fusion(bf16[2048,2048]{1,0:T(8,128)(2,1)} %get-tuple-element.350, bf16[256,2048]{1,0:T(8,128)(2,1)} %get-tuple-element.349, bf16[1,256,2048]{2,1,0:T(8,128)(2,1)S(1)} %get-tuple-element.348), kind=kOutput, calls=%fused_computation.7 | convolution fusion | flops 2149580800 | bytes 12582912 | tf_op jit(solution)/shard_map/while/body/eval_jaxpr/cond/branch_1_fun/dot_general | solution.py:78
  281.7 2.3 convolution_convert_fusion.1
  284.1 2.1 fusion.11
  286.2 17.0 %all-gather = bf16[1024,300]{0,1:T(8,128)(2,1)} all-gather(bf16[256,300]{0,1:T(8,128)(2,1)S(1)} %fusion.11), channel_id=2, replica_groups=mesh['sub'=8,'front'=4] {'front'}, dimensions={0}, use_global_device_ids=true | all-gather | bytes 768000 | tf_op jit(solution)/shard_map/all_gather | solution.py:98
  303.2 2.4 reshape.90
  305.6 1.8 reduce_sum.12
  307.5 1.7 convolution_subtract_fusion.1
  309.2 1.5 copy.10
  312.2 52.5 %all-gather.3.cloned.1.call-done = bf16[2048,256]{1,0:T(8,128)(2,1)} async-done(((bf16[64,256]{1,0:T(8,128)(2,1)}), bf16[2048,256]{1,0:T(8,128)(2,1)}) %all-gather.3.cloned.1.call-update) | async-done | bytes 1048592 | tf_op jit(solution)/shard_map/all_gather | solution.py:106
  364.7 1.5 convolution_bitcast_fusion.1
  366.2 3.8 fusion.6
  (50 shorter events, 10.0 us)
Async XLA Ops:
  7.2 276.9 %copy-start = (bf16[1,300,2048]{2,1,0:T(8,128)(2,1)S(1)}, bf16[1,300,2048]{2,1,0:T(8,128)(2,1)}, u32[]{:S(2)}) copy-start(bf16[1,300,2048]{2,1,0:T(8,128)(2,1)} %param.15) | copy-start | bytes 3686404
  7.2 357.5 %all-gather.3.cloned.1.call-start = ((), (), s32[]{:S(2)}) async-start(), calls=%async_computation | async-start | bytes 1081344 | tf_op jit(solution)/shard_map/all_gather | solution.py:106
  11.4 27.4 %collective-permute-start = (bf16[256,2048]{1,0:T(8,128)(2,1)S(1)}, bf16[256,2048]{1,0:T(8,128)(2,1)S(1)}, u32[]{:S(2)}, u32[]{:S(2)}) collective-permute-start(bf16[256,2048]{1,0:T(8,128)(2,1)S(1)} %copy.25), channel_id=1, source_target_pairs={{0,1},{1,2},{2,3},{4,5},{5,6},{6,7},{8,9},{9,10},{10,11},{12,13},{... | collective-permute-start | bytes 3145736 | tf_op jit(solution)/shard_map/while/body/eval_jaxpr/ppermute | solution.py:10
  49.7 1.0 copy-start.1
  50.8 23.1 %collective-permute-start = (bf16[256,2048]{1,0:T(8,128)(2,1)S(1)}, bf16[256,2048]{1,0:T(8,128)(2,1)S(1)}, u32[]{:S(2)}, u32[]{:S(2)}) collective-permute-start(bf16[256,2048]{1,0:T(8,128)(2,1)S(1)} %copy.25), channel_id=1, source_target_pairs={{0,1},{1,2},{2,3},{4,5},{5,6},{6,7},{8,9},{9,10},{10,11},{12,13},{... | collective-permute-start | bytes 3145736 | tf_op jit(solution)/shard_map/while/body/eval_jaxpr/ppermute | solution.py:10
  73.9 1.0 copy-start.1
  74.9 36.3 %collective-permute-start = (bf16[256,2048]{1,0:T(8,128)(2,1)S(1)}, bf16[256,2048]{1,0:T(8,128)(2,1)S(1)}, u32[]{:S(2)}, u32[]{:S(2)}) collective-permute-start(bf16[256,2048]{1,0:T(8,128)(2,1)S(1)} %copy.25), channel_id=1, source_target_pairs={{0,1},{1,2},{2,3},{4,5},{5,6},{6,7},{8,9},{9,10},{10,11},{12,13},{... | collective-permute-start | bytes 3145736 | tf_op jit(solution)/shard_map/while/body/eval_jaxpr/ppermute | solution.py:10
  111.2 1.0 copy-start.1
  112.3 24.5 %collective-permute-start = (bf16[256,2048]{1,0:T(8,128)(2,1)S(1)}, bf16[256,2048]{1,0:T(8,128)(2,1)S(1)}, u32[]{:S(2)}, u32[]{:S(2)}) collective-permute-start(bf16[256,2048]{1,0:T(8,128)(2,1)S(1)} %copy.25), channel_id=1, source_target_pairs={{0,1},{1,2},{2,3},{4,5},{5,6},{6,7},{8,9},{9,10},{10,11},{12,13},{... | collective-permute-start | bytes 3145736 | tf_op jit(solution)/shard_map/while/body/eval_jaxpr/ppermute | solution.py:10
  136.8 1.0 copy-start.1
  137.8 1.7 copy-start.2
  139.5 33.8 %collective-permute-start.1 = (bf16[256,2048]{1,0:T(8,128)(2,1)S(1)}, bf16[256,2048]{1,0:T(8,128)(2,1)}, u32[]{:S(2)}, u32[]{:S(2)}) collective-permute-start(bf16[256,2048]{1,0:T(8,128)(2,1)S(1)} %get-tuple-element.526), channel_id=1, source_target_pairs={{1,0},{2,1},{3,2},{5,4},{6,5},{7,6},{9,8},{10,9},{11,10},{13,12},{... | collective-permute-start | bytes 3145736 | tf_op jit(solution)/shard_map/while/body/eval_jaxpr/ppermute | solution.py:10
  173.3 24.2 %collective-permute-start.1 = (bf16[256,2048]{1,0:T(8,128)(2,1)S(1)}, bf16[256,2048]{1,0:T(8,128)(2,1)}, u32[]{:S(2)}, u32[]{:S(2)}) collective-permute-start(bf16[256,2048]{1,0:T(8,128)(2,1)S(1)} %get-tuple-element.526), channel_id=1, source_target_pairs={{1,0},{2,1},{3,2},{5,4},{6,5},{7,6},{9,8},{10,9},{11,10},{13,12},{... | collective-permute-start | bytes 3145736 | tf_op jit(solution)/shard_map/while/body/eval_jaxpr/ppermute | solution.py:10
  197.5 32.6 %collective-permute-start.1 = (bf16[256,2048]{1,0:T(8,128)(2,1)S(1)}, bf16[256,2048]{1,0:T(8,128)(2,1)}, u32[]{:S(2)}, u32[]{:S(2)}) collective-permute-start(bf16[256,2048]{1,0:T(8,128)(2,1)S(1)} %get-tuple-element.526), channel_id=1, source_target_pairs={{1,0},{2,1},{3,2},{5,4},{6,5},{7,6},{9,8},{10,9},{11,10},{13,12},{... | collective-permute-start | bytes 3145736 | tf_op jit(solution)/shard_map/while/body/eval_jaxpr/ppermute | solution.py:10
  230.1 45.4 %collective-permute-start.1 = (bf16[256,2048]{1,0:T(8,128)(2,1)S(1)}, bf16[256,2048]{1,0:T(8,128)(2,1)}, u32[]{:S(2)}, u32[]{:S(2)}) collective-permute-start(bf16[256,2048]{1,0:T(8,128)(2,1)S(1)} %get-tuple-element.526), channel_id=1, source_target_pairs={{1,0},{2,1},{3,2},{5,4},{6,5},{7,6},{9,8},{10,9},{11,10},{13,12},{... | collective-permute-start | bytes 3145736 | tf_op jit(solution)/shard_map/while/body/eval_jaxpr/ppermute | solution.py:10
  275.5 6.2 %copy-start.6 = (bf16[2048,2048]{1,0:T(8,128)(2,1)S(1)}, bf16[2048,2048]{1,0:T(8,128)(2,1)}, u32[]{:S(2)}) copy-start(bf16[2048,2048]{1,0:T(8,128)(2,1)} %get-tuple-element.351) | copy-start | bytes 25165828 | tf_op jit(solution)/shard_map/while/body/eval_jaxpr/cond
  281.7 2.4 copy-start.3
  286.2 21.3 %copy-start.4 = (f32[1,256,2048]{2,1,0:T(8,128)S(1)}, f32[1,256,2048]{2,1,0:T(8,128)}, u32[]{:S(2)}) copy-start(f32[1,256,2048]{2,1,0:T(8,128)} %get-tuple-element.367) | copy-start | bytes 6291460
  309.2 2.9 copy-start.5
Sparse Core Ops, SparseCore 0:
  312.2 52.3 all-gather.2
